TPU v7x, 256 devices: a whole 4x4x8 slice. The times are simulated.
256 devices in a mesh: dp: 16 (over z, core), tensor: 16 (over y, x).
Axes of the slice: x: 4, y: 4, z: 8, core: 2. Of those that a mesh axis runs over, the one named last changes fastest.
Arguments:
- hidden: bfloat16 [8192, 28672], P('dp', 'tensor'), parts along dimension 0, may hold values from -6 to 6
- down_weight: bfloat16 [28672, 4096], P('tensor'), may hold values from -0.03125 to 0.03125
Outputs:
- projected: bfloat16 [8192, 4096], P(('dp', 'tensor')), parts along dimension 0
There are 16 independent parts, one for each index of `dp`. A program takes and returns all parts, laid end to end along the dimension named above; an argument that names none is the same for every part. Nothing has to cross between parts.
All inputs are finite; a program needn't handle non-finite values.
Results may differ from a plain program's by a relative error of at most 0.019.
Values may be sent and summed in bfloat16 or wider, within the bound.
A program may use at most 128 MiB of HBM per device.

v0:
```python
import math

import jax
import jax.numpy as jnp
from jax import lax
from jax.sharding import PartitionSpec as P

FF = 28672


def from_partner(block, axis, apart):
    count = lax.axis_size(axis)
    route = []
    for low in range(count):
        high = low | 1 << apart
        if high != low and high < count:
            route += [(low, high), (high, low)]
    return lax.ppermute(block, axis, route)


def paley_table():
    modulus = 13
    residues = set((number * number % modulus for number in range(1, modulus)))
    legendre = [0.0] + [1.0 if number in residues else -1.0 for number in range(1, modulus)]
    order = modulus + 1
    conference = [[0.0] * order for row_at in range(order)]
    for col_at in range(1, order):
        conference[0][col_at] = 1.0
        conference[col_at][0] = 1.0
    for row_at in range(modulus):
        for col_at in range(modulus):
            conference[row_at + 1][col_at + 1] = legendre[(col_at - row_at) % modulus]
    plus_block = [[1.0, 1.0], [1.0, -1.0]]
    minus_block = [[1.0, -1.0], [-1.0, -1.0]]
    table = [[0.0] * (2 * order) for row_at in range(2 * order)]
    for row_at in range(order):
        for col_at in range(order):
            for inner_row in range(2):
                for inner_col in range(2):
                    value = conference[row_at][col_at] * plus_block[inner_row][inner_col]
                    if row_at == col_at:
                        value = value + minus_block[inner_row][inner_col]
                    table[2 * row_at + inner_row][2 * col_at + inner_col] = value
    return table


def walsh_table(length):
    indices = jnp.arange(length, dtype=jnp.int32)
    common = jnp.bitwise_and(indices[:, None], indices[None, :])
    parity = jnp.zeros((length, length), jnp.int32)
    for position in range(length.bit_length() - 1):
        parity = parity + jnp.bitwise_and(jnp.right_shift(common, position), 1)
    return 1.0 - 2.0 * jnp.bitwise_and(parity, 1).astype(jnp.float32)


def body(hidden, down_weight):
    group_size = lax.axis_size("tensor")
    token_count = hidden.shape[0]
    width_local = hidden.shape[1]
    walsh_local = width_local // 28
    paley = jnp.asarray(paley_table(), jnp.float32)
    factor = 1.0 / math.sqrt(FF)
    blocks = hidden.reshape(token_count, walsh_local, 28).transpose(2, 1, 0)
    local_walsh = walsh_table(walsh_local).astype(jnp.bfloat16)
    mixed = jnp.einsum("alt,lm->amt", blocks, local_walsh, preferred_element_type=jnp.float32)
    mixed = jnp.einsum("alt,ac->clt", mixed, paley, precision=lax.Precision.HIGHEST)
    device_rank = lax.axis_index("tensor")
    for position in range(group_size.bit_length() - 1):
        partner = from_partner(mixed.astype(jnp.bfloat16), "tensor", position).astype(mixed.dtype)
        upper_half = jnp.bitwise_and(jnp.right_shift(device_rank, position), 1) == 1
        mixed = jnp.where(upper_half, partner - mixed, mixed + partner)
    rotated = (
        (mixed * factor).astype(jnp.bfloat16).transpose(2, 1, 0).reshape(token_count, width_local)
    )
    return lax.psum_scatter(
        jnp.dot(rotated, down_weight, preferred_element_type=jnp.float32).astype(jnp.bfloat16),
        "tensor",
        scatter_dimension=0,
        tiled=True,
    )


def solution(mesh):
    placed = (P("dp", "tensor"), P("tensor", None))
    return jax.shard_map(
        body, mesh=mesh, in_specs=placed, out_specs=P(("dp", "tensor"), None), check_vma=False
    )
```

profile of v0, /device:TPU:160, one launch (start us, length us, event | category | flops | bytes accessed | tf_op | source)
XLA Modules:
  0.0 317.1 jit_solution(18322007535937925555)
XLA Ops:
  6.5 0.0 reduce-scatter.2.cloned.1.call-start
  6.5 3.8 %copy.16 = bf16[512,1792]{0,1:T(8,128)(2,1)} copy(bf16[512,1792]{1,0:T(8,128)(2,1)} %param.3) | data formatting | bytes 3670016 | tf_op args[0]
  10.4 2.4 reshape.6
  12.8 0.0 copy-start
  12.8 2.5 convolution_bitcast_fusion
  15.2 0.0 copy-done
  15.2 6.7 %fusion.32 = (bf16[28,64,512]{2,0,1:T(8,128)(2,1)S(1)}, f32[28,64,512]{2,0,1:T(8,128)}) fusion(f32[28,28,1]{0,1,2:T(8,128)S(1)} %copy-done, f32[28,64,512]{2,1,0:T(8,128)S(1)} %convolution_bitcast_fusion), kind=kOutput, calls=%fused_computation.41 | convolution fusion | flops 309198848 | bytes 9178176 | tf_op jit(solution)/shard_map/alt,ac->clt/dot_general | solution.py:66
  22.0 2.3 copy.19
  24.3 1.5 collective-permute-start
  25.8 40.5 %collective-permute-done = bf16[28,64,512]{2,1,0:T(8,128)(2,1)S(1)} collective-permute-done((bf16[28,64,512]{2,1,0:T(8,128)(2,1)}, bf16[28,64,512]{2,1,0:T(8,128)(2,1)S(1)}, u32[]{:S(2)}, u32[]{:S(2)}) %collective-permute-start) | collective-permute-done | bytes 1835040 | tf_op jit(solution)/shard_map/ppermute | solution.py:18
  66.2 5.6 %fusion.11 = bf16[28,64,512]{2,1,0:T(8,128)(2,1)} fusion(f32[28,64,512]{2,0,1:T(8,128)} %get-tuple-element.8, bf16[28,64,512]{2,1,0:T(8,128)(2,1)S(1)} %collective-permute-done, pred[]{:T(512)S(6)} %eq.15), kind=kLoop, calls=%fused_computation.21 | loop fusion | flops 4587520 | bytes 7340033 | tf_op jit(solution)/shard_map/convert_element_type | solution.py:69
  71.8 3.0 collective-permute-start.1
  74.8 39.7 %collective-permute-done.1 = bf16[28,64,512]{2,1,0:T(8,128)(2,1)} collective-permute-done((bf16[28,64,512]{2,1,0:T(8,128)(2,1)}, bf16[28,64,512]{2,1,0:T(8,128)(2,1)}, u32[]{:S(2)}, u32[]{:S(2)}) %collective-permute-start.1) | collective-permute-done | bytes 1835040 | tf_op jit(solution)/shard_map/ppermute | solution.py:18
  114.5 7.6 %fusion.30 = (bf16[28,64,512]{2,1,0:T(8,128)(2,1)}, f32[28,64,512]{2,1,0:T(8,128)}) fusion(f32[28,64,512]{2,0,1:T(8,128)} %get-tuple-element.8, bf16[28,64,512]{2,1,0:T(8,128)(2,1)S(1)} %collective-permute-done, pred[]{:T(512)S(6)} %eq.15, bf16[28,64,512]{2,1,0:T(8,128)(2,1)} %collective-permute-done.1, pred[]{:T(512)S(6)} %eq.14), kind=kLoop, calls=%fused_computation.40 | loop fusion | flops 8257536 | bytes 12845058 | tf_op jit(solution)/shard_map/convert_element_type | solution.py:69
  122.0 1.6 collective-permute-start.2
  123.6 38.6 %collective-permute-done.2 = bf16[28,64,512]{2,1,0:T(8,128)(2,1)S(1)} collective-permute-done((bf16[28,64,512]{2,1,0:T(8,128)(2,1)}, bf16[28,64,512]{2,1,0:T(8,128)(2,1)S(1)}, u32[]{:S(2)}, u32[]{:S(2)}) %collective-permute-start.2) | collective-permute-done | bytes 1835040 | tf_op jit(solution)/shard_map/ppermute | solution.py:18
  162.2 3.9 %fusion.8 = bf16[28,64,512]{2,1,0:T(8,128)(2,1)} fusion(f32[28,64,512]{2,1,0:T(8,128)} %get-tuple-element.6, bf16[28,64,512]{2,1,0:T(8,128)(2,1)S(1)} %collective-permute-done.2, pred[]{:T(512)S(6)} %eq.13), kind=kLoop, calls=%fused_computation.17 | loop fusion | flops 4587520 | bytes 7340033 | tf_op jit(solution)/shard_map/convert_element_type | solution.py:69
  166.2 3.2 %collective-permute-start.3 = (bf16[28,64,512]{2,1,0:T(8,128)(2,1)}, bf16[28,64,512]{2,1,0:T(8,128)(2,1)}, u32[]{:S(2)}, u32[]{:S(2)}) collective-permute-start(bf16[28,64,512]{2,1,0:T(8,128)(2,1)} %fusion.8), channel_id=1, source_target_pairs={{0,8},{8,0},{1,9},{9,1},{2,10},{10,2},{3,11},{11,3},{4,12},{12,4},... | collective-permute-start | bytes 5505032 | tf_op jit(solution)/shard_map/ppermute | solution.py:18
  169.4 37.6 %collective-permute-done.3 = bf16[28,64,512]{2,1,0:T(8,128)(2,1)} collective-permute-done((bf16[28,64,512]{2,1,0:T(8,128)(2,1)}, bf16[28,64,512]{2,1,0:T(8,128)(2,1)}, u32[]{:S(2)}, u32[]{:S(2)}) %collective-permute-start.3) | collective-permute-done | bytes 1835040 | tf_op jit(solution)/shard_map/ppermute | solution.py:18
  207.0 3.8 %fusion.9 = bf16[512,64,28]{0,1,2:T(8,128)(2,1)S(1)} fusion(f32[28,64,512]{2,1,0:T(8,128)} %get-tuple-element.6, bf16[28,64,512]{2,1,0:T(8,128)(2,1)S(1)} %collective-permute-done.2, bf16[28,64,512]{2,1,0:T(8,128)(2,1)} %collective-permute-done.3, pred[]{:T(512)S(6)} %eq.13, pred[]{:T(512)S(6)} %eq.12), kind=kLoop, calls=%fused_computation.19 | loop fusion | flops 9175040 | bytes 9175042 | tf_op jit(solution)/shard_map/transpose | solution.py:73
  210.8 1.0 copy.22
  211.8 1.5 reshape.7
  213.3 13.0 %convolution_convert_fusion = bf16[512,4096]{1,0:T(8,128)(2,1)} fusion(bf16[512,1792]{0,1:T(8,128)(2,1)} %reshape.7, bf16[1792,4096]{1,0:T(8,128)(2,1)} %param.4), kind=kOutput, calls=%fused_computation | convolution fusion | flops 7518289920 | bytes 20709376 | tf_op jit(solution)/shard_map/dot_general | solution.py:76
  226.3 0.0 reduce-scatter.2.cloned.1.call-update
  226.3 83.9 %reduce-scatter.2.cloned.1.call-done = bf16[32,4096]{1,0:T(8,128)(2,1)} async-done(((bf16[512,4096]{1,0:T(8,128)(2,1)}), bf16[32,4096]{1,0:T(8,128)(2,1)}) %reduce-scatter.2.cloned.1.call-update) | async-done | bytes 262160 | tf_op jit(solution)/shard_map/reduce_scatter | solution.py:75
Async XLA Ops:
  6.5 303.7 %reduce-scatter.2.cloned.1.call-start = ((), (), s32[]{:S(2)}) async-start(), calls=%async_computation.1 | async-start | bytes 4456448 | tf_op jit(solution)/shard_map/reduce_scatter | solution.py:75
  12.8 2.5 copy-start
  24.3 42.0 %collective-permute-start = (bf16[28,64,512]{2,1,0:T(8,128)(2,1)}, bf16[28,64,512]{2,1,0:T(8,128)(2,1)S(1)}, u32[]{:S(2)}, u32[]{:S(2)}) collective-permute-start(bf16[28,64,512]{2,1,0:T(8,128)(2,1)} %copy.19), channel_id=1, source_target_pairs={{0,1},{1,0},{2,3},{3,2},{4,5},{5,4},{6,7},{7,6},{8,9},{9,8},{10,11... | collective-permute-start | bytes 5505032 | tf_op jit(solution)/shard_map/ppermute | solution.py:18
  71.8 42.7 %collective-permute-start.1 = (bf16[28,64,512]{2,1,0:T(8,128)(2,1)}, bf16[28,64,512]{2,1,0:T(8,128)(2,1)}, u32[]{:S(2)}, u32[]{:S(2)}) collective-permute-start(bf16[28,64,512]{2,1,0:T(8,128)(2,1)} %fusion.11), channel_id=1, source_target_pairs={{0,2},{2,0},{1,3},{3,1},{4,6},{6,4},{5,7},{7,5},{8,10},{10,8},{9,1... | collective-permute-start | bytes 5505032 | tf_op jit(solution)/shard_map/ppermute | solution.py:18
  122.0 40.2 %collective-permute-start.2 = (bf16[28,64,512]{2,1,0:T(8,128)(2,1)}, bf16[28,64,512]{2,1,0:T(8,128)(2,1)S(1)}, u32[]{:S(2)}, u32[]{:S(2)}) collective-permute-start(bf16[28,64,512]{2,1,0:T(8,128)(2,1)} %get-tuple-element.5), channel_id=1, source_target_pairs={{0,4},{4,0},{1,5},{5,1},{2,6},{6,2},{3,7},{7,3},{8,12},{12,8},{9,1... | collective-permute-start | bytes 5505032 | tf_op jit(solution)/shard_map/ppermute | solution.py:18
  166.2 40.9 %collective-permute-start.3 = (bf16[28,64,512]{2,1,0:T(8,128)(2,1)}, bf16[28,64,512]{2,1,0:T(8,128)(2,1)}, u32[]{:S(2)}, u32[]{:S(2)}) collective-permute-start(bf16[28,64,512]{2,1,0:T(8,128)(2,1)} %fusion.8), channel_id=1, source_target_pairs={{0,8},{8,0},{1,9},{9,1},{2,10},{10,2},{3,11},{11,3},{4,12},{12,4},... | collective-permute-start | bytes 5505032 | tf_op jit(solution)/shard_map/ppermute | solution.py:18
Sparse Core Ops, SparseCore 0:
  226.4 83.7 reduce-scatter.1
where the time goes:
time: 319 us; the launch traced here: 317 us
  waiting for transfers between devices  240 us (75%)
  matrix products  22.2 us (7%)
  other arithmetic  20.8 us (7%)
  between operations  13.4 us (4%)
  local copies, waits for them, and re-layouts  11 us (3%)
  starting transfers between devices  9.3 us (3%)
    ppermute x4, waiting for transfers between devices, from_partner(): return lax.ppermute(block, axis, route)  156 us
    reduce_scatter x1, waiting for transfers between devices, body(): lax.psum_scatter(jnp.dot(rotated, down_weight, preferred_element_type=jnp...  83.9 us
    convert_element_type x3, other arithmetic, body(): mixed.astype(jnp.bfloat16)  17.1 us
    dot_general x1, matrix products, body(): jnp.dot(rotated, down_weight, preferred_element_type=jnp.float32)  13 us
    ppermute x4, starting transfers between devices, from_partner(): return lax.ppermute(block, axis, route)  9.29 us
    dot_general x1, matrix products, body(): jnp.einsum('alt,ac->clt', mixed, paley, precision=lax.Precision.HIGHEST)  6.74 us
  transfers between devices with their start and end apart: 5, of which 5 were waited for; matrix products, arithmetic and copies ran while one was open for 0% of the time, Pallas kernels for 0%

commit v1 on v0

v1 whole, which is shorter than its diff:
```python
import functools
import math

import jax
import jax.numpy as jnp
import ml_dtypes
import numpy as np
from jax import lax
from jax.experimental import pallas as pl
from jax.experimental.pallas import tpu as pltpu
from jax.sharding import PartitionSpec as P

FF = 28672
SCALE = 1.0 / math.sqrt(FF)
MESH = pl.DeviceIdType.MESH
HALF = 896
ROWS = 16
CHUNKS = 2
QUARTER = 1024


def paley_table():
    modulus = 13
    residues = set(number * number % modulus for number in range(1, modulus))
    legendre = [0.0] + [1.0 if number in residues else -1.0 for number in range(1, modulus)]
    order = modulus + 1
    conference = np.zeros((order, order), np.float32)
    conference[0, 1:] = 1.0
    conference[1:, 0] = 1.0
    for row in range(modulus):
        for col in range(modulus):
            conference[row + 1, col + 1] = legendre[(col - row) % modulus]
    plus_block = np.array([[1.0, 1.0], [1.0, -1.0]], np.float32)
    minus_block = np.array([[1.0, -1.0], [-1.0, -1.0]], np.float32)
    return np.kron(conference, plus_block) + np.kron(np.eye(order, dtype=np.float32), minus_block)


def local_rotation():
    walsh = np.ones((1, 1), np.float32)
    for _ in range(5):
        walsh = np.kron(np.array([[1.0, 1.0], [1.0, -1.0]], np.float32), walsh)
    return np.kron(walsh, paley_table()).astype(ml_dtypes.bfloat16)


def walsh_blocks(values):
    values = list(values)
    apart = 1
    while apart < len(values):
        for low in range(len(values)):
            if low & apart == 0:
                a, b = values[low], values[low + apart]
                values[low], values[low + apart] = a + b, a - b
        apart *= 2
    return values


def kernel(
    hidden, weight, rotation, out,
    w_vmem, k_vmem, mid1, gath, turned, mid2, tokens, product, partial, recv1, recv2, recv3, recv4,
    load_sem, a2a_send, a2a_recv, rs_send, rs_recv,
):
    me = lax.axis_index("tensor")
    y, x = me // 4, me % 4

    def at(y_to, x_to):
        return {"tensor": y_to * 4 + x_to}

    def flip(v, by):
        if by == 1:
            return v + 1 - 2 * (v % 2)
        if by == 3:
            return 3 - v
        return (v + 2) % 4

    barrier = pltpu.get_barrier_semaphore()
    for k in (1, 2, 3):
        pl.semaphore_signal(barrier, inc=1, device_id=at(y, (x + k) % 4), device_id_type=MESH)
        pl.semaphore_signal(barrier, inc=1, device_id=at((y + k) % 4, x), device_id_type=MESH)

    load_k = pltpu.make_async_copy(rotation, k_vmem, load_sem.at[0])
    load_w = pltpu.make_async_copy(weight, w_vmem, load_sem.at[1])

    sends = []

    def push(src, dst, send_sem, recv_sem, to):
        copy = pltpu.make_async_remote_copy(
            src_ref=src, dst_ref=dst, send_sem=send_sem, recv_sem=recv_sem,
            device_id=to, device_id_type=MESH,
        )
        copy.start()

    def landed(buf, sem):
        pltpu.make_async_copy(buf, buf, sem).wait()

    def leg1(turn, c, sources, mid):
        for k in (1, 3, 2, 0):
            for half in (0, 1):
                recv = a2a_recv.at[turn, 0, half, c]
                send = a2a_send.at[turn, 0, half, c]
                if half == 0:
                    to = (x + k) % 4
                    src, dst, dev = sources(half, c).at[:, to], mid.at[half, c, x], at(y, to)
                else:
                    to = (y + k) % 4
                    src, dst, dev = sources(half, c).at[to], mid.at[half, c, y], at(to, x)
                if k == 0:
                    pltpu.make_async_copy(src, dst, recv).start()
                else:
                    push(src, dst, send, recv, dev)
        for half in (0, 1):
            sends.append((mid.at[half, c, pl.ds(0, 3)], a2a_send.at[turn, 0, half, c]))

    def leg2(turn, c, mid, end):
        for half in (0, 1):
            landed(mid.at[half, c], a2a_recv.at[turn, 0, half, c])
            for k in (1, 3, 2, 0):
                recv = a2a_recv.at[turn, 1, half, c]
                send = a2a_send.at[turn, 1, half, c]
                if half == 0:
                    to = (y + k) % 4
                    src, dst, dev = mid.at[half, c, :, to], end.at[half, c, y], at(to, x)
                else:
                    to = (x + k) % 4
                    src, dst, dev = mid.at[half, c, :, to], end.at[half, c, :, x], at(y, to)
                if k == 0:
                    pltpu.make_async_copy(src, dst, recv).start()
                else:
                    push(src, dst, send, recv, dev)
            sends.append((mid.at[half, c, pl.ds(0, 3)], a2a_send.at[turn, 1, half, c]))

    def arrive(turn, c, end):
        for half in (0, 1):
            landed(end.at[half, c], a2a_recv.at[turn, 1, half, c])

    def from_hidden(half, c):
        return hidden.at[:, :, pl.ds(ROWS * c, ROWS), pl.ds(HALF * half, HALF)]

    def from_turned(half, c):
        return turned.at[half, c]

    def rotate(c):
        for half in (0, 1):
            block = gath[half, c].reshape(16 * ROWS, HALF)
            product[half] = jnp.dot(block, k_vmem[...], preferred_element_type=jnp.float32)

        def columns(j, carry):
            lanes = pl.ds(pl.multiple_of(j * 128, 128), 128)
            for half in (0, 1):
                values = []
                for s in range(16):
                    a = product[0, pl.ds(s * ROWS, ROWS), lanes]
                    b = product[1, pl.ds(s * ROWS, ROWS), lanes]
                    values.append(a + b if half == 0 else a - b)
                for t, value in enumerate(walsh_blocks(values)):
                    turned[half, c, t // 4, t % 4, :, lanes] = (value * SCALE).astype(jnp.bfloat16)
            return carry

        lax.fori_loop(0, HALF // 128, columns, 0)

    def multiply(c, q):
        def tile(j, carry):
            cols = pl.ds(pl.multiple_of(q * QUARTER + j * 256, 256), 256)
            total = jnp.dot(
                tokens[0, c].reshape(16 * ROWS, HALF), w_vmem[pl.ds(0, HALF), cols],
                preferred_element_type=jnp.float32,
            ) + jnp.dot(
                tokens[1, c].reshape(16 * ROWS, HALF), w_vmem[pl.ds(HALF, HALF), cols],
                preferred_element_type=jnp.float32,
            )
            here = pl.ds(pl.multiple_of(j * 256, 256), 256)
            partial[c, q, :, :, :, here] = total.astype(jnp.bfloat16).reshape(4, 4, ROWS, 256)
            return carry

        lax.fori_loop(0, QUARTER // 256, tile, 0)

    def order(q):
        return (q < 2), ((1, 3) if q % 2 == 0 else (3, 1))

    def peer(along_x, by):
        return at(y, flip(x, by)) if along_x else at(flip(y, by), x)

    def rs1(c, q):
        x_first, (p1, p2) = order(q)
        for slot, by in ((0, p1), (1, 2)):
            src = partial.at[c, q, :, flip(x, by)] if x_first else partial.at[c, q, flip(y, by)]
            push(src, recv1.at[c, q, slot], rs_send.at[c, q, 0], rs_recv.at[c, q, 0], peer(x_first, p1))
        sends.append((recv1.at[c, q], rs_send.at[c, q, 0]))

    def rs2(c, q):
        x_first, (p1, p2) = order(q)
        landed(recv1.at[c, q], rs_recv.at[c, q, 0])
        for slot, by in ((1, p2), (0, 0)):
            pos = flip(x if x_first else y, by) if by else (x if x_first else y)
            ref = partial.at[c, q, :, pos] if x_first else partial.at[c, q, pos]
            ref[...] = (ref[...].astype(jnp.float32) + recv1[c, q, slot].astype(jnp.float32)).astype(jnp.bfloat16)
            if by:
                push(ref, recv2.at[c, q], rs_send.at[c, q, 1], rs_recv.at[c, q, 1], peer(x_first, p2))
                sends.append((recv2.at[c, q], rs_send.at[c, q, 1]))

    def rs3(c, q):
        x_first, (p1, p2) = order(q)
        landed(recv2.at[c, q], rs_recv.at[c, q, 1])
        ref = partial.at[c, q, :, x] if x_first else partial.at[c, q, y]
        ref[...] = (ref[...].astype(jnp.float32) + recv2[c, q].astype(jnp.float32)).astype(jnp.bfloat16)
        for slot, by in ((0, p1), (1, 2)):
            src = partial.at[c, q, flip(y, by), x] if x_first else partial.at[c, q, y, flip(x, by)]
            push(src, recv3.at[c, q, slot], rs_send.at[c, q, 2], rs_recv.at[c, q, 2], peer(not x_first, p1))
        sends.append((recv3.at[c, q], rs_send.at[c, q, 2]))

    def rs4(c, q):
        x_first, (p1, p2) = order(q)
        landed(recv3.at[c, q], rs_recv.at[c, q, 2])
        ref = partial.at[c, q, flip(y, p2), x] if x_first else partial.at[c, q, y, flip(x, p2)]
        ref[...] = (ref[...].astype(jnp.float32) + recv3[c, q, 1].astype(jnp.float32)).astype(jnp.bfloat16)
        push(ref, recv4.at[c, q], rs_send.at[c, q, 3], rs_recv.at[c, q, 3], peer(not x_first, p2))
        sends.append((recv4.at[c, q], rs_send.at[c, q, 3]))

    def finish(c, q):
        landed(recv4.at[c, q], rs_recv.at[c, q, 3])
        total = (
            partial[c, q, y, x].astype(jnp.float32)
            + recv3[c, q, 0].astype(jnp.float32)
            + recv4[c, q].astype(jnp.float32)
        )
        out[pl.ds(ROWS * c, ROWS), pl.ds(QUARTER * q, QUARTER)] = total.astype(jnp.bfloat16)

    pl.semaphore_wait(barrier, 6)
    for c in range(CHUNKS):
        leg1(0, c, from_hidden, mid1)
    load_k.start()
    load_w.start()
    for c in range(CHUNKS):
        leg2(0, c, mid1, gath)
    load_k.wait()
    for c in range(CHUNKS):
        arrive(0, c, gath)
        rotate(c)
        leg1(1, c, from_turned, mid2)
    for c in range(CHUNKS):
        leg2(1, c, mid2, tokens)
    load_w.wait()
    for c in range(CHUNKS):
        arrive(1, c, tokens)
        for q in range(4):
            multiply(c, q)
            rs1(c, q)
    for step in (rs2, rs3, rs4, finish):
        for c in range(CHUNKS):
            for q in range(4):
                step(c, q)
    for ref, sem in sends:
        landed(ref, sem)


def body(hidden, down_weight):
    any_space = pl.BlockSpec(memory_space=pl.ANY)
    legs = (2, CHUNKS, 4, 4, ROWS, HALF)
    bf16 = jnp.bfloat16
    return pl.pallas_call(
        kernel,
        out_shape=jax.ShapeDtypeStruct((32, 4096), bf16),
        in_specs=[any_space] * 3,
        out_specs=pl.BlockSpec(memory_space=pltpu.VMEM),
        scratch_shapes=[
            pltpu.VMEM((2 * HALF, 4096), bf16),
            pltpu.VMEM((HALF, HALF), bf16),
            pltpu.VMEM(legs, bf16),
            pltpu.VMEM(legs, bf16),
            pltpu.VMEM(legs, bf16),
            pltpu.VMEM(legs, bf16),
            pltpu.VMEM(legs, bf16),
            pltpu.VMEM((2, 16 * ROWS, HALF), jnp.float32),
            pltpu.VMEM((CHUNKS, 4, 4, 4, ROWS, QUARTER), bf16),
            pltpu.VMEM((CHUNKS, 4, 2, 4, ROWS, QUARTER), bf16),
            pltpu.VMEM((CHUNKS, 4, 4, ROWS, QUARTER), bf16),
            pltpu.VMEM((CHUNKS, 4, 2, ROWS, QUARTER), bf16),
            pltpu.VMEM((CHUNKS, 4, ROWS, QUARTER), bf16),
            pltpu.SemaphoreType.DMA((2,)),
            pltpu.SemaphoreType.DMA((2, 2, 2, CHUNKS)),
            pltpu.SemaphoreType.DMA((2, 2, 2, CHUNKS)),
            pltpu.SemaphoreType.DMA((CHUNKS, 4, 4)),
            pltpu.SemaphoreType.DMA((CHUNKS, 4, 4)),
        ],
        compiler_params=pltpu.CompilerParams(
            collective_id=0, has_side_effects=True, vmem_limit_bytes=60 << 20
        ),
    )(hidden.reshape(4, 4, 32, 2 * HALF), down_weight, jnp.asarray(local_rotation()))


def solution(mesh):
    placed = (P("dp", "tensor"), P("tensor", None))
    return jax.shard_map(
        body, mesh=mesh, in_specs=placed, out_specs=P(("dp", "tensor"), None), check_vma=False
    )
```

time: 319 us -> 79.9 us (0.25)
  waiting for transfers between devices: 240 us -> 0 us
  Pallas kernels: 0 us -> 78.1 us
  matrix products: 22.2 us -> 0 us
  other arithmetic: 20.8 us -> 0 us
  between operations: 13.4 us -> 0.01 us
  local copies, waits for them, and re-layouts: 11 us -> 1.67 us
  starting transfers between devices: 9.3 us -> 0 us
    ppermute x4 -> x0, waiting for transfers between devices: 156 us -> none  [from_partner(): return lax.ppermute(block, axis, route)]
    reduce_scatter x1 -> x0, waiting for transfers between devices: 83.9 us -> none  [body(): lax.psum_scatter(jnp.dot(rotated, down_weight, preferred_element_type=jnp...]
    pallas_call x0 -> x1, Pallas kernels: none -> 78.1 us  [body(): pl.pallas_call(kernel, out_shape=jax.ShapeDtypeStruct((32, 4096), bf16),...]
    dot_general x3 -> x0, matrix products: 22.2 us -> none  [the longest x1 13 us: body(): jnp.dot(rotated, down_weight, preferred_element_type=jnp.float32)]
    convert_element_type x3 -> x0, other arithmetic: 17.1 us -> none  [body(): mixed.astype(jnp.bfloat16)]
    ppermute x4 -> x0, starting transfers between devices: 9.29 us -> none  [from_partner(): return lax.ppermute(block, axis, route)]
    reshape x2 -> x0, local copies, waits for them, and re-layouts: 3.85 us -> none  [the longest x1 2.4 us: body(): blocks = hidden.reshape(token_count, walsh_local, 28).transpose(2, 1, 0)]
    transpose x1 -> x0, other arithmetic: 3.77 us -> none  [body(): (mixed * factor).astype(jnp.bfloat16).transpose(2, 1, 0)]
  transfers between devices with their start and end apart: 5 -> 0, of which waited for: 5 -> 0; matrix products, arithmetic and copies ran while one was open for 0% -> 0% of each run, Pallas kernels for 0% -> 0%
where the time goes in v1:
time: 79.9 us; the launch traced here: 79.8 us
  Pallas kernels  78.1 us (98%)
  local copies, waits for them, and re-layouts  1.67 us (2%)
    pallas_call x1, Pallas kernels, body(): pl.pallas_call(kernel, out_shape=jax.ShapeDtypeStruct((32, 4096), bf16),...  78.1 us
    unnamed x1, local copies, waits for them, and re-layouts  1.67 us

profile of v1, /device:TPU:160, one launch (start us, length us, event | category | flops | bytes accessed | tf_op | source)
XLA Modules:
  0.0 79.8 jit_solution(1998290195435864358)
XLA Ops:
  0.0 78.1 %shard_map.37 = bf16[32,4096]{1,0:T(8,128)(2,1)} custom-call(bf16[4,4,32,1792]{3,2,1,0:T(8,128)(2,1)} %bitcast.1, bf16[1792,4096]{1,0:T(8,128)(2,1)} %weight.1, bf16[896,896]{1,0:T(8,128)(2,1)} %constant.2.clone.rotation), custom_call_target="tpu_custom_call" | custom-call | tf_op jit(solution)/shard_map/pallas_call | solution.py:259
  78.1 1.7 %copy.5 = bf16[32,4096]{1,0:T(8,128)(2,1)} copy(bf16[32,4096]{1,0:T(8,128)(2,1)} %shard_map.37) | data formatting | bytes 524288

commit v2 on v1

--- a/solution.py
+++ b/solution.py
@@ -16,7 +16,8 @@
 HALF = 896
 ROWS = 16
 CHUNKS = 2
-QUARTER = 1024
+PIECES = 8
+QUARTER = 4096 // PIECES
 
 
 def paley_table():
@@ -174,7 +175,7 @@
         lax.fori_loop(0, QUARTER // 256, tile, 0)
 
     def order(q):
-        return (q < 2), ((1, 3) if q % 2 == 0 else (3, 1))
+        return (q % 2 == 0), ((1, 3) if q % 4 < 2 else (3, 1))
 
     def peer(along_x, by):
         return at(y, flip(x, by)) if along_x else at(flip(y, by), x)
@@ -241,12 +242,12 @@
     load_w.wait()
     for c in range(CHUNKS):
         arrive(1, c, tokens)
-        for q in range(4):
+        for q in range(PIECES):
             multiply(c, q)
             rs1(c, q)
     for step in (rs2, rs3, rs4, finish):
         for c in range(CHUNKS):
-            for q in range(4):
+            for q in range(PIECES):
                 step(c, q)
     for ref, sem in sends:
         landed(ref, sem)
@@ -270,16 +271,16 @@
             pltpu.VMEM(legs, bf16),
             pltpu.VMEM(legs, bf16),
             pltpu.VMEM((2, 16 * ROWS, HALF), jnp.float32),
-            pltpu.VMEM((CHUNKS, 4, 4, 4, ROWS, QUARTER), bf16),
-            pltpu.VMEM((CHUNKS, 4, 2, 4, ROWS, QUARTER), bf16),
-            pltpu.VMEM((CHUNKS, 4, 4, ROWS, QUARTER), bf16),
-            pltpu.VMEM((CHUNKS, 4, 2, ROWS, QUARTER), bf16),
-            pltpu.VMEM((CHUNKS, 4, ROWS, QUARTER), bf16),
+            pltpu.VMEM((CHUNKS, PIECES, 4, 4, ROWS, QUARTER), bf16),
+            pltpu.VMEM((CHUNKS, PIECES, 2, 4, ROWS, QUARTER), bf16),
+            pltpu.VMEM((CHUNKS, PIECES, 4, ROWS, QUARTER), bf16),
+            pltpu.VMEM((CHUNKS, PIECES, 2, ROWS, QUARTER), bf16),
+            pltpu.VMEM((CHUNKS, PIECES, ROWS, QUARTER), bf16),
             pltpu.SemaphoreType.DMA((2,)),
             pltpu.SemaphoreType.DMA((2, 2, 2, CHUNKS)),
             pltpu.SemaphoreType.DMA((2, 2, 2, CHUNKS)),
-            pltpu.SemaphoreType.DMA((CHUNKS, 4, 4)),
-            pltpu.SemaphoreType.DMA((CHUNKS, 4, 4)),
+            pltpu.SemaphoreType.DMA((CHUNKS, PIECES, 4)),
+            pltpu.SemaphoreType.DMA((CHUNKS, PIECES, 4)),
         ],
         compiler_params=pltpu.CompilerParams(
             collective_id=0, has_side_effects=True, vmem_limit_bytes=60 << 20

time: 79.9 us -> 77.8 us (0.974)
  Pallas kernels: 78.1 us -> 76.1 us
    pallas_call x1, Pallas kernels: 78.1 us -> 76.1 us  [body(): pl.pallas_call(kernel, out_shape=jax.ShapeDtypeStruct((32, 4096), bf16),...]
where the time goes in v2:
time: 77.8 us; the launch traced here: 77.7 us
  Pallas kernels  76.1 us (98%)
  local copies, waits for them, and re-layouts  1.67 us (2%)
    pallas_call x1, Pallas kernels, body(): pl.pallas_call(kernel, out_shape=jax.ShapeDtypeStruct((32, 4096), bf16),...  76.1 us
    unnamed x1, local copies, waits for them, and re-layouts  1.67 us

profile of v2, /device:TPU:160, one launch (start us, length us, event | category | flops | bytes accessed | tf_op | source)
XLA Modules:
  0.0 77.7 jit_solution(6510260752997465785)
XLA Ops:
  0.0 76.1 %shard_map.37 = bf16[32,4096]{1,0:T(8,128)(2,1)} custom-call(bf16[4,4,32,1792]{3,2,1,0:T(8,128)(2,1)} %bitcast.1, bf16[1792,4096]{1,0:T(8,128)(2,1)} %weight.1, bf16[896,896]{1,0:T(8,128)(2,1)} %constant.2.clone.rotation), custom_call_target="tpu_custom_call" | custom-call | tf_op jit(solution)/shard_map/pallas_call | solution.py:260
  76.1 1.7 %copy.5 = bf16[32,4096]{1,0:T(8,128)(2,1)} copy(bf16[32,4096]{1,0:T(8,128)(2,1)} %shard_map.37) | data formatting | bytes 524288

commit v3 on v2

--- a/solution.py
+++ b/solution.py
@@ -160,19 +160,14 @@
 
     def multiply(c, q):
         def tile(j, carry):
-            cols = pl.ds(pl.multiple_of(q * QUARTER + j * 256, 256), 256)
-            total = jnp.dot(
-                tokens[0, c].reshape(16 * ROWS, HALF), w_vmem[pl.ds(0, HALF), cols],
-                preferred_element_type=jnp.float32,
-            ) + jnp.dot(
-                tokens[1, c].reshape(16 * ROWS, HALF), w_vmem[pl.ds(HALF, HALF), cols],
-                preferred_element_type=jnp.float32,
-            )
-            here = pl.ds(pl.multiple_of(j * 256, 256), 256)
-            partial[c, q, :, :, :, here] = total.astype(jnp.bfloat16).reshape(4, 4, ROWS, 256)
+            cols = pl.ds(pl.multiple_of(q * QUARTER + j * 512, 512), 512)
+            block = jnp.concatenate([tokens[half, c].reshape(16 * ROWS, HALF) for half in (0, 1)], axis=1)
+            total = jnp.dot(block, w_vmem[:, cols], preferred_element_type=jnp.float32)
+            here = pl.ds(pl.multiple_of(j * 512, 512), 512)
+            partial[c, q, :, :, :, here] = total.astype(jnp.bfloat16).reshape(4, 4, ROWS, 512)
             return carry
 
-        lax.fori_loop(0, QUARTER // 256, tile, 0)
+        lax.fori_loop(0, QUARTER // 512, tile, 0)
 
     def order(q):
         return (q % 2 == 0), ((1, 3) if q % 4 < 2 else (3, 1))

time: 77.8 us -> 74.8 us (0.961)
  Pallas kernels: 76.1 us -> 73 us
    pallas_call x1, Pallas kernels: 76.1 us -> 73 us  [body(): pl.pallas_call(kernel, out_shape=jax.ShapeDtypeStruct((32, 4096), bf16),...]
where the time goes in v3:
time: 74.8 us; the launch traced here: 74.7 us
  Pallas kernels  73 us (98%)
  local copies, waits for them, and re-layouts  1.67 us (2%)
    pallas_call x1, Pallas kernels, body(): pl.pallas_call(kernel, out_shape=jax.ShapeDtypeStruct((32, 4096), bf16),...  73 us
    unnamed x1, local copies, waits for them, and re-layouts  1.67 us

profile of v3, /device:TPU:160, one launch (start us, length us, event | category | flops | bytes accessed | tf_op | source)
XLA Modules:
  0.0 74.7 jit_solution(11422386136268177819)
XLA Ops:
  0.0 73.0 %shard_map.37 = bf16[32,4096]{1,0:T(8,128)(2,1)} custom-call(bf16[4,4,32,1792]{3,2,1,0:T(8,128)(2,1)} %bitcast.1, bf16[1792,4096]{1,0:T(8,128)(2,1)} %weight.1, bf16[896,896]{1,0:T(8,128)(2,1)} %constant.2.clone.rotation), custom_call_target="tpu_custom_call" | custom-call | tf_op jit(solution)/shard_map/pallas_call | solution.py:255
  73.1 1.7 %copy.5 = bf16[32,4096]{1,0:T(8,128)(2,1)} copy(bf16[32,4096]{1,0:T(8,128)(2,1)} %shard_map.37) | data formatting | bytes 524288
